TPU v7x, 256 devices: a whole 4x4x8 slice. The times are simulated.
256 devices in a mesh: node: 64 (over z, y, core), state: 4 (over x).
Axes of the slice: x: 4, y: 4, z: 8, core: 2. Of those that a mesh axis runs over, the one named last changes fastest.
Arguments:
- block: bfloat16 [64, 2097152], P('state', 'node'), may hold values from -6 to 6
- connectivity: int32 [125, 32768], P(None, 'node'), may hold values from 0 to 49151, as said below
- potential: float32 [125, 32768], P(None, 'node'), may hold values from 0.1 to 3
- cell_matrix: bfloat16 [125, 125], replicated, as said below
Outputs:
- orthonormal: bfloat16 [64, 2097152], P('state', 'node')
- factor: float32 [64, 64], replicated
Inputs may be any that keep to these rules, and one draw needn't show every extreme that they name: `connectivity`: in each slab, numbers below 8192 are the previous slab's last 8192 nodes and numbers from 40960 on are the next slab's first nodes. The numbers of the slab's k-th cell (k from 0) lie in k * 96 to k * 96 + 2 * 96 - 1, those of its last cell in k * 96 to k * 96 + 95; each cell reaches the lower end of its range. `cell_matrix`: Symmetric.
All inputs are finite; a program needn't handle non-finite values.
Results may differ from a plain program's by a relative error of at most 0.015.
Values may be sent and summed in bfloat16 or wider, within the bound.
No kernel may reach another device: no remote copies, remote signals or barrier semaphores. Data moves between devices by JAX's collectives and lax.ppermute only.
A program may use at most 64 MiB of HBM per device.

v0:
```python
import jax
import jax.numpy as jnp
from jax import lax
from jax.sharding import PartitionSpec as P

CENTER = 3.0
HALF_WIDTH = 3.0


def extended(block, sides, width):
    for axis, dim in sides:
        count = lax.axis_size(axis)
        forward = [(i, i + 1) for i in range(count - 1)]
        backward = [(target, source) for source, target in forward]
        low = lax.ppermute(
            lax.slice_in_dim(block, block.shape[dim] - width, None, axis=dim), axis, forward
        )
        high = lax.ppermute(lax.slice_in_dim(block, 0, width, axis=dim), axis, backward)
        block = jnp.concatenate([low, block, high], axis=dim)
    return block


def passed_along(block, axis, distance):
    devices = range(lax.axis_size(axis))
    route = [(i - distance, i) for i in devices if i - distance in devices]
    return lax.ppermute(block, axis, route)


def cell_terms(window, connectivity, potential, cell_matrix):
    states = window.shape[0]
    cells = connectivity.shape[1]
    stride = window.shape[1] // cells
    segments = window.reshape(states, cells, stride)
    following = jnp.concatenate(
        [segments[:, 1:], jnp.zeros((states, 1, stride), segments.dtype)], axis=1
    )
    paired = jnp.concatenate([segments, following], axis=2)
    offsets = jnp.arange(cells, dtype=jnp.int32) * stride
    local_links = connectivity - offsets[None, :]
    columns = jnp.arange(2 * stride, dtype=jnp.int32)
    group = min(cells, 128)
    pieces = []
    for first_cell in range(0, cells, group):
        links = local_links[:, first_cell : first_cell + group]
        picker = links[:, :, None] == columns[None, None, :]
        picker_half = picker.astype(jnp.bfloat16)
        part_pair = paired[:, first_cell : first_cell + group]
        values = jnp.einsum(
            "skn,jkn->sjk", part_pair, picker_half, preferred_element_type=jnp.float32
        )
        mixed = jnp.einsum(
            "ij,sjk->sik",
            cell_matrix,
            values.astype(jnp.bfloat16),
            preferred_element_type=jnp.float32,
        )
        mixed = mixed + potential[None, :, first_cell : first_cell + group] * values
        spread = jnp.einsum(
            "sjk,jkn->skn", mixed, picker.astype(jnp.float32), precision=lax.Precision.HIGHEST
        )
        pieces.append(spread)
    spread = jnp.concatenate(pieces, axis=1)
    lower = spread[:, :, :stride]
    upper = spread[:, :, stride:]
    shifted = jnp.concatenate([jnp.zeros((states, 1, stride), jnp.float32), upper[:, :-1]], axis=1)
    return (lower + shifted).reshape(states, cells * stride)


def operate(field, connectivity, potential, cell_matrix):
    owned = field.shape[1]
    margin = owned // 4
    window = extended(field, (("node", 1),), margin)
    summed = cell_terms(window, connectivity, potential, cell_matrix)
    result = summed[:, margin : margin + owned]
    from_above = passed_along(summed[:, :margin].astype(jnp.bfloat16), "node", -1).astype(
        jnp.float32
    )
    from_below = passed_along(summed[:, margin + owned :].astype(jnp.bfloat16), "node", 1).astype(
        jnp.float32
    )
    result = result.at[:, owned - margin :].add(from_above)
    result = result.at[:, :margin].add(from_below)
    return result


def factorize(intersection):
    factor = jnp.linalg.cholesky(intersection)
    identity = jnp.eye(intersection.shape[0], dtype=factor.dtype)
    inverse = lax.linalg.triangular_solve(factor, identity, left_side=True, lower=True).astype(
        jnp.bfloat16
    )
    return (factor, inverse)


def per_device(block, connectivity, potential, cell_matrix):
    start = block.astype(jnp.float32)
    image = operate(block, connectivity, potential, cell_matrix)
    first = ((image - CENTER * start) / HALF_WIDTH).astype(jnp.bfloat16)
    image = operate(first, connectivity, potential, cell_matrix)
    second = (2.0 * (image - CENTER * first.astype(jnp.float32)) / HALF_WIDTH - start).astype(
        jnp.bfloat16
    )
    total_nodes = block.shape[1] * lax.axis_size("node")
    panel = lax.all_gather(second, "state", axis=0, tiled=True)
    partial_intersection = jnp.einsum("an,bn->ab", panel, panel, preferred_element_type=jnp.float32)
    intersection = lax.psum(partial_intersection, "node") / total_nodes
    factor, inverse = factorize(intersection)
    rows = second.shape[0]
    mine = lax.dynamic_slice_in_dim(inverse, lax.axis_index("state") * rows, rows, 0)
    orthonormal = jnp.dot(mine, panel, preferred_element_type=jnp.float32).astype(jnp.bfloat16)
    return (orthonormal, factor)


def solution(mesh):
    return jax.shard_map(
        per_device,
        mesh=mesh,
        in_specs=(P("state", "node"), P(None, "node"), P(None, "node"), P()),
        out_specs=(P("state", "node"), P()),
        check_vma=False,
    )
```

profile of v0, /device:TPU:2, one launch (start us, length us, event | category | flops | bytes accessed | tf_op | source)
XLA Modules:
  0.0 566.9 jit_solution(16091128970053678684)
XLA Ops:
  8.4 1.8 collective-permute-start
  10.1 1.3 collective-permute-start.1
  16.8 3.2 reshape.132
  20.0 1.4 copy.18
  21.7 2.8 fusion.34
  24.5 3.0 fusion.123
  28.4 4.3 fusion.122
  33.6 4.3 fusion.121
  38.2 1.5 copy.37
  39.8 4.2 fusion.120
  44.3 1.4 copy.39
  45.8 11.6 %fusion.42 = f32[16,128,192]{2,0,1:T(8,128)S(1)} fusion(s32[125,128]{0,1:T(8,128)S(1)} %copy.16, f32[16,128,125]{2,0,1:T(8,128)S(1)} %copy.33, f32[16,125,128]{1,0,2:T(8,128)} %get-tuple-element.75, f32[125,128]{0,1:T(8,128)} %copy.19), kind=kOutput, calls=%fused_computation.59 | convolution fusion | flops 593408000 | bytes 3748864 | tf_op jit(solution)/shard_map/sjk,jkn->skn/dot_general | solution.py:58
  57.4 9.9 %fusion.44 = f32[16,128,192]{2,0,1:T(8,128)S(1)} fusion(s32[125,128]{0,1:T(8,128)S(1)} %copy-done.11, f32[16,128,125]{2,0,1:T(8,128)S(1)} %copy.35, f32[16,125,128]{1,0,2:T(8,128)S(1)} %copy-done.19, f32[125,128]{0,1:T(8,128)S(1)} %copy-done.14), kind=kOutput, calls=%fused_computation.61 | convolution fusion | flops 593408000 | bytes 3748864 | tf_op jit(solution)/shard_map/sjk,jkn->skn/dot_general | solution.py:58
  67.3 10.0 %fusion.46 = f32[16,128,192]{2,0,1:T(8,128)S(1)} fusion(s32[125,128]{0,1:T(8,128)S(1)} %copy.22, f32[16,128,125]{2,0,1:T(8,128)S(1)} %copy-done.7, f32[16,125,128]{1,0,2:T(8,128)S(1)} %copy-done.20, f32[125,128]{0,1:T(8,128)S(1)} %copy.23), kind=kOutput, calls=%fused_computation.63 | convolution fusion | flops 593408000 | bytes 3748864 | tf_op jit(solution)/shard_map/sjk,jkn->skn/dot_general | solution.py:58
  77.3 9.8 %fusion.48 = f32[16,128,192]{2,0,1:T(8,128)S(1)} fusion(s32[125,128]{0,1:T(8,128)S(1)} %copy.24, f32[16,128,125]{2,0,1:T(8,128)S(1)} %copy-done.9, f32[16,125,128]{1,0,2:T(8,128)S(1)} %copy-done.21, f32[125,128]{0,1:T(8,128)S(1)} %copy.25), kind=kOutput, calls=%fused_computation.65 | convolution fusion | flops 593408000 | bytes 3748864 | tf_op jit(solution)/shard_map/sjk,jkn->skn/dot_general | solution.py:58
  88.2 2.3 fusion.37
  90.5 3.2 copy.26
  93.8 4.0 reshape.133
  98.0 1.3 collective-permute-start.2
  100.0 6.8 %collective-permute-start.3 = (bf16[16,8192]{1,0:T(8,128)(2,1)S(1)}, bf16[16,8192]{1,0:T(8,128)(2,1)S(1)}, u32[]{:S(2)}, u32[]{:S(2)}) collective-permute-start(bf16[16,8192]{1,0:T(8,128)(2,1)S(1)} %get-tuple-element.54), channel_id=1, source_target_pairs={{0,4},{4,8},{8,12},{12,16},{16,20},{20,24},{24,28},{28,32},{32,36}... | collective-permute-start | bytes 786440 | tf_op jit(solution)/shard_map/ppermute | solution.py:26
  109.2 5.8 %collective-permute-start.4 = (bf16[16,8192]{1,0:T(8,128)(2,1)S(1)}, bf16[16,8192]{1,0:T(8,128)(2,1)S(1)}, u32[]{:S(2)}, u32[]{:S(2)}) collective-permute-start(bf16[16,8192]{1,0:T(8,128)(2,1)S(1)} %get-tuple-element.56), channel_id=1, source_target_pairs={{0,4},{4,8},{8,12},{12,16},{16,20},{20,24},{24,28},{28,32},{32,36}... | collective-permute-start | bytes 786440 | tf_op jit(solution)/shard_map/ppermute | solution.py:15
  115.0 1.3 collective-permute-start.5
  116.3 4.1 collective-permute-done.5
  121.7 3.2 reshape.134
  124.9 1.4 copy.28
  126.6 3.0 fusion.35
  129.6 3.0 fusion.127
  132.7 3.0 fusion.126
  135.7 3.0 fusion.125
  138.7 3.0 fusion.124
  142.0 1.5 copy.41
  143.8 1.4 copy.43
  147.0 11.7 %fusion.43 = f32[16,128,192]{2,0,1:T(8,128)S(1)} fusion(s32[125,128]{0,1:T(8,128)S(1)} %copy.16, f32[16,128,125]{2,0,1:T(8,128)} %copy.41, f32[16,125,128]{1,0,2:T(8,128)} %get-tuple-element.83, f32[125,128]{0,1:T(8,128)} %copy.19), kind=kOutput, calls=%fused_computation.60 | convolution fusion | flops 593408000 | bytes 3748864 | tf_op jit(solution)/shard_map/sjk,jkn->skn/dot_general | solution.py:58
  158.8 9.9 %fusion.45 = f32[16,128,192]{2,0,1:T(8,128)S(1)} fusion(s32[125,128]{0,1:T(8,128)S(1)} %copy-done.13, f32[16,128,125]{2,0,1:T(8,128)S(1)} %copy-done.8, f32[16,125,128]{1,0,2:T(8,128)S(1)} %copy-done.18, f32[125,128]{0,1:T(8,128)S(1)} %copy-done.15), kind=kOutput, calls=%fused_computation.62 | convolution fusion | flops 593408000 | bytes 3748864 | tf_op jit(solution)/shard_map/sjk,jkn->skn/dot_general | solution.py:58
  168.7 10.0 %fusion.47 = f32[16,128,192]{2,0,1:T(8,128)S(1)} fusion(s32[125,128]{0,1:T(8,128)S(1)} %copy.22, f32[16,128,125]{2,0,1:T(8,128)S(1)} %copy.45, f32[16,125,128]{1,0,2:T(8,128)S(1)} %copy-done.17, f32[125,128]{0,1:T(8,128)S(1)} %copy.23), kind=kOutput, calls=%fused_computation.64 | convolution fusion | flops 593408000 | bytes 3748864 | tf_op jit(solution)/shard_map/sjk,jkn->skn/dot_general | solution.py:58
  178.7 9.8 %fusion.49 = f32[16,128,192]{2,0,1:T(8,128)S(1)} fusion(s32[125,128]{0,1:T(8,128)S(1)} %copy.24, f32[16,128,125]{2,0,1:T(8,128)S(1)} %copy.47, f32[16,125,128]{1,0,2:T(8,128)S(1)} %copy-done.16, f32[125,128]{0,1:T(8,128)S(1)} %copy.25), kind=kOutput, calls=%fused_computation.66 | convolution fusion | flops 593408000 | bytes 3748864 | tf_op jit(solution)/shard_map/sjk,jkn->skn/dot_general | solution.py:58
  189.6 2.3 fusion.36
  192.0 3.2 copy.29
  195.2 4.0 reshape.135
  199.4 1.4 collective-permute-start.6
  201.0 7.3 %collective-permute-start.7 = (bf16[16,8192]{1,0:T(8,128)(2,1)S(1)}, bf16[16,8192]{1,0:T(8,128)(2,1)S(1)}, u32[]{:S(2)}, u32[]{:S(2)}) collective-permute-start(bf16[16,8192]{1,0:T(8,128)(2,1)S(1)} %get-tuple-element.52), channel_id=1, source_target_pairs={{0,4},{4,8},{8,12},{12,16},{16,20},{20,24},{24,28},{28,32},{32,36}... | collective-permute-start | bytes 786440 | tf_op jit(solution)/shard_map/ppermute | solution.py:26
  210.3 1.4 fusion.41
  211.7 75.3 %all-gather.2.cloned.1.call-done = bf16[64,32768]{1,0:T(8,128)(2,1)} async-done(((bf16[16,32768]{1,0:T(8,128)(2,1)}), bf16[64,32768]{1,0:T(8,128)(2,1)}) %all-gather.2.cloned.1.call-update) | async-done | bytes 4194320 | tf_op jit(solution)/shard_map/all_gather | solution.py:104
  287.0 4.7 fusion.128
  291.7 251.0 %psum.7 = f32[64,64]{0,1:T(8,128)S(1)} all-reduce(f32[64,64]{0,1:T(8,128)S(1)} %fusion.128), channel_id=1, replica_groups=mesh['node'=64,'state'=4] {'node'}, use_global_device_ids=true, to_apply=%region_1.0 | all-reduce | flops 4096 | bytes 32768 | tf_op jit(solution)/shard_map/psum | solution.py:106
  542.8 5.8 %cholesky.17 = f32[64,64]{1,0:T(8,128)S(1)} custom-call(f32[64,64]{1,0:T(8,128)S(1)} %fusion.104), custom_call_target="Cholesky" | custom-call | tf_op jit(solution)/shard_map/jit(cholesky)/cholesky | solution.py:87
  550.6 4.9 custom-call.6
  555.8 3.8 convolution_convert_fusion
  (104 shorter events, 23.2 us)
Async XLA Ops:
  7.2 20.4 %copy-start = (bf16[125,125]{1,0:T(8,128)(2,1)S(1)}, bf16[125,125]{1,0:T(8,128)(2,1)}, u32[]{:S(2)}) copy-start(bf16[125,125]{1,0:T(8,128)(2,1)} %param.15) | copy-start | bytes 93754
  7.2 8.4 %copy-start.1 = (bf16[16,32768]{1,0:T(8,128)(2,1)S(1)}, bf16[16,32768]{1,0:T(8,128)(2,1)}, u32[]{:S(2)}) copy-start(bf16[16,32768]{1,0:T(8,128)(2,1)} %param.12) | copy-start | bytes 3145732
  7.2 279.8 %all-gather.2.cloned.1.call-start = ((), (), s32[]{:S(2)}) async-start(), calls=%async_computation | async-start | bytes 5242880 | tf_op jit(solution)/shard_map/all_gather | solution.py:104
  8.4 7.1 %collective-permute-start = (bf16[16,8192]{1,0:T(8,128)(2,1)S(1)}, bf16[16,8192]{1,0:T(8,128)(2,1)S(1)}, u32[]{:S(2)}, u32[]{:S(2)}) collective-permute-start(bf16[16,8192]{1,0:T(8,128)(2,1)S(1)} %get-tuple-element.58), channel_id=1, source_target_pairs={{0,4},{4,8},{8,12},{12,16},{16,20},{20,24},{24,28},{28,32},{32,36}... | collective-permute-start | bytes 786440 | tf_op jit(solution)/shard_map/ppermute | solution.py:15
  10.1 5.4 collective-permute-start.1
  14.4 14.1 %copy-start.10 = (s32[125,128]{0,1:T(8,128)}, s32[125,128]{0,1:T(8,128)S(1)}, u32[]{:S(2)}) copy-start(s32[125,128]{0,1:T(8,128)S(1)} %copy.20) | copy-start | bytes 192004
  24.5 3.0 copy-start.6
  45.8 11.6 %copy-start.11 = (s32[125,128]{0,1:T(8,128)S(1)}, s32[125,128]{0,1:T(8,128)}, u32[]{:S(2)}) copy-start(s32[125,128]{0,1:T(8,128)} %copy-done.10) | copy-start | bytes 192004
  45.8 11.6 %copy-start.14 = (f32[125,128]{0,1:T(8,128)S(1)}, f32[125,128]{0,1:T(8,128)}, u32[]{:S(2)}) copy-start(f32[125,128]{0,1:T(8,128)} %copy.21) | copy-start | bytes 192004
  45.8 11.6 %copy-start.19 = (f32[16,125,128]{1,0,2:T(8,128)S(1)}, f32[16,125,128]{1,0,2:T(8,128)}, u32[]{:S(2)}) copy-start(f32[16,125,128]{1,0,2:T(8,128)} %get-tuple-element.73) | copy-start | bytes 3072004
  57.4 9.9 %copy-start.7 = (f32[16,128,125]{2,0,1:T(8,128)S(1)}, f32[16,128,125]{2,0,1:T(8,128)}, u32[]{:S(2)}) copy-start(f32[16,128,125]{2,0,1:T(8,128)} %copy.37) | copy-start | bytes 3072004
  57.4 9.9 %copy-start.20 = (f32[16,125,128]{1,0,2:T(8,128)S(1)}, f32[16,125,128]{1,0,2:T(8,128)}, u32[]{:S(2)}) copy-start(f32[16,125,128]{1,0,2:T(8,128)} %get-tuple-element.71) | copy-start | bytes 3072004
  67.3 10.0 %copy-start.9 = (f32[16,128,125]{2,0,1:T(8,128)S(1)}, f32[16,128,125]{2,0,1:T(8,128)}, u32[]{:S(2)}) copy-start(f32[16,128,125]{2,0,1:T(8,128)} %copy.39) | copy-start | bytes 3072004
  67.3 10.0 %copy-start.21 = (f32[16,125,128]{1,0,2:T(8,128)S(1)}, f32[16,125,128]{1,0,2:T(8,128)}, u32[]{:S(2)}) copy-start(f32[16,125,128]{1,0,2:T(8,128)} %get-tuple-element.69) | copy-start | bytes 3072004
  98.0 8.9 %collective-permute-start.2 = (bf16[16,8192]{1,0:T(8,128)(2,1)S(1)}, bf16[16,8192]{1,0:T(8,128)(2,1)S(1)}, u32[]{:S(2)}, u32[]{:S(2)}) collective-permute-start(bf16[16,8192]{1,0:T(8,128)(2,1)S(1)} %get-tuple-element.55), channel_id=1, source_target_pairs={{4,0},{8,4},{12,8},{16,12},{20,16},{24,20},{28,24},{32,28},{36,32}... | collective-permute-start | bytes 786440 | tf_op jit(solution)/shard_map/ppermute | solution.py:26
  99.9 8.9 %copy-start.2 = (bf16[16,32768]{1,0:T(8,128)(2,1)S(1)}, bf16[16,32768]{1,0:T(8,128)(2,1)}, u32[]{:S(2)}) copy-start(bf16[16,32768]{1,0:T(8,128)(2,1)} %param.12) | copy-start | bytes 3145732
  100.0 8.0 %collective-permute-start.3 = (bf16[16,8192]{1,0:T(8,128)(2,1)S(1)}, bf16[16,8192]{1,0:T(8,128)(2,1)S(1)}, u32[]{:S(2)}, u32[]{:S(2)}) collective-permute-start(bf16[16,8192]{1,0:T(8,128)(2,1)S(1)} %get-tuple-element.54), channel_id=1, source_target_pairs={{0,4},{4,8},{8,12},{12,16},{16,20},{20,24},{24,28},{28,32},{32,36}... | collective-permute-start | bytes 786440 | tf_op jit(solution)/shard_map/ppermute | solution.py:26
  109.2 11.3 %copy-start.4 = (bf16[16,32768]{1,0:T(8,128)(2,1)}, bf16[16,32768]{1,0:T(8,128)(2,1)S(1)}, u32[]{:S(2)}) copy-start(bf16[16,32768]{1,0:T(8,128)(2,1)S(1)} %fusion.40) | copy-start | bytes 3145732
  109.2 7.1 %collective-permute-start.4 = (bf16[16,8192]{1,0:T(8,128)(2,1)S(1)}, bf16[16,8192]{1,0:T(8,128)(2,1)S(1)}, u32[]{:S(2)}, u32[]{:S(2)}) collective-permute-start(bf16[16,8192]{1,0:T(8,128)(2,1)S(1)} %get-tuple-element.56), channel_id=1, source_target_pairs={{0,4},{4,8},{8,12},{12,16},{16,20},{20,24},{24,28},{28,32},{32,36}... | collective-permute-start | bytes 786440 | tf_op jit(solution)/shard_map/ppermute | solution.py:15
  115.0 5.4 collective-permute-start.5
  129.6 3.0 copy-start.12
  147.0 11.7 %copy-start.8 = (f32[16,128,125]{2,0,1:T(8,128)S(1)}, f32[16,128,125]{2,0,1:T(8,128)}, u32[]{:S(2)}) copy-start(f32[16,128,125]{2,0,1:T(8,128)} %copy.43) | copy-start | bytes 3072004
  147.0 11.7 %copy-start.13 = (s32[125,128]{0,1:T(8,128)S(1)}, s32[125,128]{0,1:T(8,128)}, u32[]{:S(2)}) copy-start(s32[125,128]{0,1:T(8,128)} %copy-done.10) | copy-start | bytes 192004
  147.0 11.7 %copy-start.15 = (f32[125,128]{0,1:T(8,128)S(1)}, f32[125,128]{0,1:T(8,128)}, u32[]{:S(2)}) copy-start(f32[125,128]{0,1:T(8,128)} %copy.21) | copy-start | bytes 192004
  147.0 11.7 %copy-start.18 = (f32[16,125,128]{1,0,2:T(8,128)S(1)}, f32[16,125,128]{1,0,2:T(8,128)}, u32[]{:S(2)}) copy-start(f32[16,125,128]{1,0,2:T(8,128)} %get-tuple-element.81) | copy-start | bytes 3072004
  158.8 9.9 %copy-start.17 = (f32[16,125,128]{1,0,2:T(8,128)S(1)}, f32[16,125,128]{1,0,2:T(8,128)}, u32[]{:S(2)}) copy-start(f32[16,125,128]{1,0,2:T(8,128)} %get-tuple-element.79) | copy-start | bytes 3072004
  168.6 10.1 %copy-start.16 = (f32[16,125,128]{1,0,2:T(8,128)S(1)}, f32[16,125,128]{1,0,2:T(8,128)}, u32[]{:S(2)}) copy-start(f32[16,125,128]{1,0,2:T(8,128)} %get-tuple-element.77) | copy-start | bytes 3072004
  199.4 10.9 %copy-start.3 = (bf16[16,32768]{1,0:T(8,128)(2,1)S(1)}, bf16[16,32768]{1,0:T(8,128)(2,1)}, u32[]{:S(2)}) copy-start(bf16[16,32768]{1,0:T(8,128)(2,1)} %param.12) | copy-start | bytes 3145732
  199.4 10.9 %copy-start.5 = (bf16[16,32768]{1,0:T(8,128)(2,1)S(1)}, bf16[16,32768]{1,0:T(8,128)(2,1)}, u32[]{:S(2)}) copy-start(bf16[16,32768]{1,0:T(8,128)(2,1)} %copy-done.4) | copy-start | bytes 3145732
  199.4 8.9 %collective-permute-start.6 = (bf16[16,8192]{1,0:T(8,128)(2,1)S(1)}, bf16[16,8192]{1,0:T(8,128)(2,1)S(1)}, u32[]{:S(2)}, u32[]{:S(2)}) collective-permute-start(bf16[16,8192]{1,0:T(8,128)(2,1)S(1)} %get-tuple-element.53), channel_id=1, source_target_pairs={{4,0},{8,4},{12,8},{16,12},{20,16},{24,20},{28,24},{32,28},{36,32}... | collective-permute-start | bytes 786440 | tf_op jit(solution)/shard_map/ppermute | solution.py:26
  201.0 8.4 %collective-permute-start.7 = (bf16[16,8192]{1,0:T(8,128)(2,1)S(1)}, bf16[16,8192]{1,0:T(8,128)(2,1)S(1)}, u32[]{:S(2)}, u32[]{:S(2)}) collective-permute-start(bf16[16,8192]{1,0:T(8,128)(2,1)S(1)} %get-tuple-element.52), channel_id=1, source_target_pairs={{0,4},{4,8},{8,12},{12,16},{16,20},{20,24},{24,28},{28,32},{32,36}... | collective-permute-start | bytes 786440 | tf_op jit(solution)/shard_map/ppermute | solution.py:26
Sparse Core Ops, SparseCore 0:
  211.9 75.0 all-gather.1
where the time goes:
time: 572 us; the launch traced here: 567 us
  blocking collectives  251 us (44%)
  matrix products  122 us (21%)
  waiting for transfers between devices  81.5 us (14%)
  local copies, waits for them, and re-layouts  37.1 us (6%)
  other arithmetic  33.2 us (6%)
  starting transfers between devices  27 us (5%)
  between operations  15.2 us (3%)
    psum x1, blocking collectives, per_device(): intersection = lax.psum(partial_intersection, 'node') / total_nodes  251 us
    dot_general x8, matrix products, cell_terms(): jnp.einsum('sjk,jkn->skn', mixed, picker.astype(jnp.float32), precision=l...  82.7 us
    all_gather x1, waiting for transfers between devices, per_device(): panel = lax.all_gather(second, 'state', axis=0, tiled=True)  75.3 us
    dot_general x8, matrix products, cell_terms(): jnp.einsum('skn,jkn->sjk', part_pair, picker_half, preferred_element_type...  27.9 us
    ppermute x4, starting transfers between devices, passed_along(): return lax.ppermute(block, axis, route)  16.9 us
  transfers between devices with their start and end apart: 9, of which 4 were waited for; matrix products, arithmetic and copies ran while one was open for 1% of the time, Pallas kernels for 0%

commit v1 on v0

--- a/solution.py
+++ b/solution.py
@@ -103,7 +103,7 @@
     total_nodes = block.shape[1] * lax.axis_size("node")
     panel = lax.all_gather(second, "state", axis=0, tiled=True)
     partial_intersection = jnp.einsum("an,bn->ab", panel, panel, preferred_element_type=jnp.float32)
-    intersection = lax.psum(partial_intersection, "node") / total_nodes
+    intersection = jnp.sum(lax.all_gather(partial_intersection, "node"), axis=0) / total_nodes
     factor, inverse = factorize(intersection)
     rows = second.shape[0]
     mine = lax.dynamic_slice_in_dim(inverse, lax.axis_index("state") * rows, rows, 0)

time: 572 us -> 458 us (0.80)
  blocking collectives: 251 us -> 0 us
  waiting for transfers between devices: 81.5 us -> 160 us
  local copies, waits for them, and re-layouts: 37.1 us -> 68.8 us
  other arithmetic: 33.2 us -> 48.5 us
  matrix products: 122 us -> 132 us
    psum x1 -> x0, blocking collectives: 251 us -> none  [per_device(): intersection = lax.psum(partial_intersection, 'node') / total_nodes]
    all_gather x0 -> x1, waiting for transfers between devices: none -> 78.4 us  [per_device(): lax.all_gather(partial_intersection, 'node')]
    add x0 -> x8, local copies, waits for them, and re-layouts: none -> 14.1 us  [cell_terms(): mixed = mixed + potential[None, :, first_cell:first_cell + group] * values]
    add x0 -> x6, other arithmetic: none -> 13.1 us  [cell_terms(): mixed = mixed + potential[None, :, first_cell:first_cell + group] * values]
    dot_general x0 -> x8, local copies, waits for them, and re-layouts: none -> 9.82 us  [cell_terms(): jnp.einsum('skn,jkn->sjk', part_pair, picker_half, preferred_element_type...]
    dot_general x8, matrix products: 82.7 us -> 92.3 us  [cell_terms(): jnp.einsum('sjk,jkn->skn', mixed, picker.astype(jnp.float32), precision=l...]
    dot_general x8, local copies, waits for them, and re-layouts: 8.11 us -> 14.2 us  [cell_terms(): jnp.einsum('ij,sjk->sik', cell_matrix, values.astype(jnp.bfloat16), prefe...]
  transfers between devices with their start and end apart: 9 -> 10, of which waited for: 4 -> 5; matrix products, arithmetic and copies ran while one was open for 1% -> 1% of each run, Pallas kernels for 0% -> 0%
where the time goes in v1:
time: 458 us; the launch traced here: 452 us
  waiting for transfers between devices  160 us (35%)
  matrix products  132 us (29%)
  local copies, waits for them, and re-layouts  68.8 us (15%)
  other arithmetic  48.5 us (11%)
  starting transfers between devices  27.5 us (6%)
  between operations  15 us (3%)
    dot_general x8, matrix products, cell_terms(): jnp.einsum('sjk,jkn->skn', mixed, picker.astype(jnp.float32), precision=l...  92.3 us
    all_gather x1, waiting for transfers between devices, per_device(): lax.all_gather(partial_intersection, 'node')  78.4 us
    all_gather x1, waiting for transfers between devices, per_device(): panel = lax.all_gather(second, 'state', axis=0, tiled=True)  75.2 us
    dot_general x8, matrix products, cell_terms(): jnp.einsum('skn,jkn->sjk', part_pair, picker_half, preferred_element_type...  24.8 us
    ppermute x4, starting transfers between devices, passed_along(): return lax.ppermute(block, axis, route)  17.3 us
    dot_general x8, local copies, waits for them, and re-layouts, cell_terms(): jnp.einsum('ij,sjk->sik', cell_matrix, values.astype(jnp.bfloat16), prefe...  14.2 us
    add x8, local copies, waits for them, and re-layouts, cell_terms(): mixed = mixed + potential[None, :, first_cell:first_cell + group] * values  14.1 us
    add x6, other arithmetic, cell_terms(): mixed = mixed + potential[None, :, first_cell:first_cell + group] * values  13.1 us
  transfers between devices with their start and end apart: 10, of which 5 were waited for; matrix products, arithmetic and copies ran while one was open for 1% of the time, Pallas kernels for 0%

profile of v1, /device:TPU:2, one launch (start us, length us, event | category | flops | bytes accessed | tf_op | source)
XLA Modules:
  0.0 451.6 jit_solution(8125960439727185281)
XLA Ops:
  16.4 3.2 reshape.132
  21.3 3.1 fusion.34
  24.5 2.0 copy-done.10
  26.4 2.0 fusion.15
  31.1 10.7 %fusion.42 = f32[16,128,192]{2,0,1:T(8,128)S(1)} fusion(f32[16,125,128]{1,0,2:T(8,128)S(1)} %copy.67, s32[125,128]{0,1:T(8,128)} %copy-done.19), kind=kOutput, calls=%fused_computation.59 | convolution fusion | flops 592896000 | bytes 2660864 | tf_op jit(solution)/shard_map/sjk,jkn->skn/dot_general | solution.py:58
  41.8 4.4 fusion.11
  46.2 1.9 copy.69
  49.5 2.6 copy.71
  52.1 2.3 bitcast_add_fusion.6
  56.3 12.1 %fusion.44 = f32[16,128,192]{2,0,1:T(8,128)} fusion(f32[16,125,128]{1,0,2:T(8,128)S(1)} %copy.72, s32[125,128]{0,1:T(8,128)} %copy.68), kind=kOutput, calls=%fused_computation.61 | convolution fusion | flops 592896000 | bytes 2660864 | tf_op jit(solution)/shard_map/sjk,jkn->skn/dot_general | solution.py:58
  68.4 4.2 fusion.7
  72.6 2.3 copy.74
  76.3 2.6 copy.76
  78.9 2.3 bitcast_add_fusion.5
  83.1 12.1 %fusion.46 = f32[16,128,192]{2,0,1:T(8,128)} fusion(f32[16,125,128]{1,0,2:T(8,128)S(1)} %copy.77, s32[125,128]{0,1:T(8,128)} %copy.73), kind=kOutput, calls=%fused_computation.63 | convolution fusion | flops 592896000 | bytes 2660864 | tf_op jit(solution)/shard_map/sjk,jkn->skn/dot_general | solution.py:58
  95.2 4.2 fusion.3
  102.7 2.8 copy.81
  105.5 2.3 bitcast_add_fusion.4
  109.7 9.8 %fusion.48 = f32[16,128,192]{2,0,1:T(8,128)S(1)} fusion(f32[16,125,128]{1,0,2:T(8,128)S(1)} %copy.82, s32[125,128]{0,1:T(8,128)S(1)} %copy.78), kind=kOutput, calls=%fused_computation.65 | convolution fusion | flops 592896000 | bytes 2660864 | tf_op jit(solution)/shard_map/sjk,jkn->skn/dot_general | solution.py:58
  120.7 2.1 fusion.37
  122.7 3.2 copy.83
  126.0 4.0 reshape.133
  132.3 7.2 %collective-permute-start.3 = (bf16[16,8192]{1,0:T(8,128)(2,1)S(1)}, bf16[16,8192]{1,0:T(8,128)(2,1)S(1)}, u32[]{:S(2)}, u32[]{:S(2)}) collective-permute-start(bf16[16,8192]{1,0:T(8,128)(2,1)S(1)} %get-tuple-element.54), channel_id=1, source_target_pairs={{0,4},{4,8},{8,12},{12,16},{16,20},{20,24},{24,28},{28,32},{32,36}... | collective-permute-start | bytes 786440 | tf_op jit(solution)/shard_map/ppermute | solution.py:26
  141.8 5.8 %collective-permute-start.4 = (bf16[16,8192]{1,0:T(8,128)(2,1)S(1)}, bf16[16,8192]{1,0:T(8,128)(2,1)S(1)}, u32[]{:S(2)}, u32[]{:S(2)}) collective-permute-start(bf16[16,8192]{1,0:T(8,128)(2,1)S(1)} %get-tuple-element.56), channel_id=1, source_target_pairs={{0,4},{4,8},{8,12},{12,16},{16,20},{20,24},{24,28},{28,32},{32,36}... | collective-permute-start | bytes 786440 | tf_op jit(solution)/shard_map/ppermute | solution.py:15
  149.0 4.1 collective-permute-done.5
  154.4 3.2 reshape.134
  159.3 3.0 fusion.35
  162.3 2.0 fusion.13
  164.3 2.0 fusion.9
  166.3 3.0 fusion.5
  169.4 3.0 fusion.1
  177.4 2.9 bitcast_add_fusion.2
  182.2 12.2 %fusion.43 = f32[16,128,192]{2,0,1:T(8,128)} fusion(f32[16,125,128]{1,0,2:T(8,128)S(1)} %copy.89, s32[125,128]{0,1:T(8,128)} %copy-done.19), kind=kOutput, calls=%fused_computation.60 | convolution fusion | flops 592896000 | bytes 2660864 | tf_op jit(solution)/shard_map/sjk,jkn->skn/dot_general | solution.py:58
  196.1 12.7 %fusion.45 = f32[16,128,192]{2,0,1:T(8,128)} fusion(f32[16,125,128]{1,0,2:T(8,128)} %copy.93, s32[125,128]{0,1:T(8,128)S(1)} %copy-done.18), kind=kOutput, calls=%fused_computation.62 | convolution fusion | flops 592896000 | bytes 2660864 | tf_op jit(solution)/shard_map/sjk,jkn->skn/dot_general | solution.py:58
  213.9 3.0 bitcast_add_fusion
  216.8 2.7 copy.97
  219.6 11.5 %fusion.47 = f32[16,128,192]{2,0,1:T(8,128)S(1)} fusion(f32[16,125,128]{1,0,2:T(8,128)} %copy.97, s32[125,128]{0,1:T(8,128)S(1)} %copy-done.15), kind=kOutput, calls=%fused_computation.64 | convolution fusion | flops 592896000 | bytes 2660864 | tf_op jit(solution)/shard_map/sjk,jkn->skn/dot_general | solution.py:58
  232.7 11.2 %fusion.49 = f32[16,128,192]{2,0,1:T(8,128)S(1)} fusion(f32[16,125,128]{1,0,2:T(8,128)} %copy.101, s32[125,128]{0,1:T(8,128)S(1)} %copy.78), kind=kOutput, calls=%fused_computation.66 | convolution fusion | flops 592896000 | bytes 2660864 | tf_op jit(solution)/shard_map/sjk,jkn->skn/dot_general | solution.py:58
  245.0 2.1 fusion.36
  247.0 3.2 copy.102
  250.3 4.2 reshape.135
  256.3 7.3 %collective-permute-start.7 = (bf16[16,8192]{1,0:T(8,128)(2,1)S(1)}, bf16[16,8192]{1,0:T(8,128)(2,1)S(1)}, u32[]{:S(2)}, u32[]{:S(2)}) collective-permute-start(bf16[16,8192]{1,0:T(8,128)(2,1)S(1)} %get-tuple-element.52), channel_id=1, source_target_pairs={{0,4},{4,8},{8,12},{12,16},{16,20},{20,24},{24,28},{28,32},{32,36}... | collective-permute-start | bytes 786440 | tf_op jit(solution)/shard_map/ppermute | solution.py:26
  267.0 75.2 %all-gather.4.cloned.1.call-done = bf16[64,32768]{1,0:T(8,128)(2,1)} async-done(((bf16[16,32768]{1,0:T(8,128)(2,1)}), bf16[64,32768]{1,0:T(8,128)(2,1)}) %all-gather.4.cloned.1.call-update) | async-done | bytes 4194320 | tf_op jit(solution)/shard_map/all_gather | solution.py:104
  342.2 5.3 %fusion.96 = f32[64,64]{1,0:T(8,128)} fusion(bf16[64,32768]{1,0:T(8,128)(2,1)} %all-gather.4.cloned.1.call-done), kind=kOutput, calls=%fused_computation.154 | convolution fusion | flops 268435456 | bytes 4210688 | tf_op jit(solution)/shard_map/an,bn->ab/dot_general | solution.py:105
  347.5 78.4 %all-gather.6.cloned.1.call-done = f32[4096,64]{1,0:T(8,128)} async-done(((f32[64,64]{1,0:T(8,128)}), f32[4096,64]{1,0:T(8,128)}) %all-gather.6.cloned.1.call-update) | async-done | bytes 1048592 | tf_op jit(solution)/shard_map/all_gather | solution.py:106
  427.9 5.8 %cholesky.17 = f32[64,64]{1,0:T(8,128)S(1)} custom-call(f32[64,64]{1,0:T(8,128)S(1)} %fusion.80), custom_call_target="Cholesky" | custom-call | tf_op jit(solution)/shard_map/jit(cholesky)/cholesky | solution.py:87
  435.6 4.9 %custom-call.6 = f32[1,64,64]{1,2,0:T(8,128)S(1)} custom-call(f32[1,64,64]{2,1,0:T(8,128)S(1)} %get-tuple-element.50), custom_call_target="InvertDiagBlocksLowerTriangular" | custom-call | tf_op jit(solution)/shard_map/triangular_solve | solution.py:89
  440.8 3.8 convolution_convert_fusion
  (130 shorter events, 60.5 us)
Async XLA Ops:
  7.2 22.1 %copy-start = (bf16[125,125]{1,0:T(8,128)(2,1)S(1)}, bf16[125,125]{1,0:T(8,128)(2,1)}, u32[]{:S(2)}) copy-start(bf16[125,125]{1,0:T(8,128)(2,1)} %param.15) | copy-start | bytes 93754
  7.2 7.9 %copy-start.1 = (bf16[16,32768]{1,0:T(8,128)(2,1)S(1)}, bf16[16,32768]{1,0:T(8,128)(2,1)}, u32[]{:S(2)}) copy-start(bf16[16,32768]{1,0:T(8,128)(2,1)} %param.12) | copy-start | bytes 3145732
  7.2 335.0 %all-gather.4.cloned.1.call-start = ((), (), s32[]{:S(2)}) async-start(), calls=%async_computation | async-start | bytes 5242880 | tf_op jit(solution)/shard_map/all_gather | solution.py:104
  8.4 6.7 %collective-permute-start = (bf16[16,8192]{1,0:T(8,128)(2,1)S(1)}, bf16[16,8192]{1,0:T(8,128)(2,1)S(1)}, u32[]{:S(2)}, u32[]{:S(2)}) collective-permute-start(bf16[16,8192]{1,0:T(8,128)(2,1)S(1)} %get-tuple-element.58), channel_id=1, source_target_pairs={{0,4},{4,8},{8,12},{12,16},{16,20},{20,24},{24,28},{28,32},{32,36}... | collective-permute-start | bytes 786440 | tf_op jit(solution)/shard_map/ppermute | solution.py:15
  10.1 5.0 %collective-permute-start.1 = (bf16[16,8192]{1,0:T(8,128)(2,1)S(1)}, bf16[16,8192]{1,0:T(8,128)(2,1)S(1)}, u32[]{:S(2)}, u32[]{:S(2)}) collective-permute-start(bf16[16,8192]{1,0:T(8,128)(2,1)S(1)} %get-tuple-element.59), channel_id=1, source_target_pairs={{4,0},{8,4},{12,8},{16,12},{20,16},{24,20},{28,24},{32,28},{36,32}... | collective-permute-start | bytes 786440 | tf_op jit(solution)/shard_map/ppermute | solution.py:18
  12.6 11.9 %copy-start.19 = (s32[125,128]{0,1:T(8,128)}, s32[125,128]{0,1:T(8,128)S(1)}, u32[]{:S(2)}) copy-start(s32[125,128]{0,1:T(8,128)S(1)} %copy.61) | copy-start | bytes 192004
  24.5 2.0 copy-start.10
  31.1 10.7 %copy-start.16 = (s32[125,128]{0,1:T(8,128)S(1)}, s32[125,128]{0,1:T(8,128)}, u32[]{:S(2)}) copy-start(s32[125,128]{0,1:T(8,128)} %copy.68) | copy-start | bytes 192004
  56.3 12.1 %copy-start.13 = (s32[125,128]{0,1:T(8,128)S(1)}, s32[125,128]{0,1:T(8,128)}, u32[]{:S(2)}) copy-start(s32[125,128]{0,1:T(8,128)} %copy.73) | copy-start | bytes 192004
  109.7 9.9 %copy-start.8 = (f32[16,128,192]{2,0,1:T(8,128)S(1)}, f32[16,128,192]{2,0,1:T(8,128)}, u32[]{:S(2)}) copy-start(f32[16,128,192]{2,0,1:T(8,128)} %fusion.44) | copy-start | bytes 4718596
  109.7 9.9 %copy-start.9 = (f32[16,128,192]{2,0,1:T(8,128)S(1)}, f32[16,128,192]{2,0,1:T(8,128)}, u32[]{:S(2)}) copy-start(f32[16,128,192]{2,0,1:T(8,128)} %fusion.46) | copy-start | bytes 4718596
  130.2 9.3 %collective-permute-start.2 = (bf16[16,8192]{1,0:T(8,128)(2,1)S(1)}, bf16[16,8192]{1,0:T(8,128)(2,1)S(1)}, u32[]{:S(2)}, u32[]{:S(2)}) collective-permute-start(bf16[16,8192]{1,0:T(8,128)(2,1)S(1)} %get-tuple-element.55), channel_id=1, source_target_pairs={{4,0},{8,4},{12,8},{16,12},{20,16},{24,20},{28,24},{32,28},{36,32}... | collective-permute-start | bytes 786440 | tf_op jit(solution)/shard_map/ppermute | solution.py:26
  132.1 9.3 %copy-start.2 = (bf16[16,32768]{1,0:T(8,128)(2,1)S(1)}, bf16[16,32768]{1,0:T(8,128)(2,1)}, u32[]{:S(2)}) copy-start(bf16[16,32768]{1,0:T(8,128)(2,1)} %param.12) | copy-start | bytes 3145732
  132.3 8.4 %collective-permute-start.3 = (bf16[16,8192]{1,0:T(8,128)(2,1)S(1)}, bf16[16,8192]{1,0:T(8,128)(2,1)S(1)}, u32[]{:S(2)}, u32[]{:S(2)}) collective-permute-start(bf16[16,8192]{1,0:T(8,128)(2,1)S(1)} %get-tuple-element.54), channel_id=1, source_target_pairs={{0,4},{4,8},{8,12},{12,16},{16,20},{20,24},{24,28},{28,32},{32,36}... | collective-permute-start | bytes 786440 | tf_op jit(solution)/shard_map/ppermute | solution.py:26
  141.8 11.3 %copy-start.4 = (bf16[16,32768]{1,0:T(8,128)(2,1)}, bf16[16,32768]{1,0:T(8,128)(2,1)S(1)}, u32[]{:S(2)}) copy-start(bf16[16,32768]{1,0:T(8,128)(2,1)S(1)} %fusion.40) | copy-start | bytes 3145732
  141.8 7.1 %collective-permute-start.4 = (bf16[16,8192]{1,0:T(8,128)(2,1)S(1)}, bf16[16,8192]{1,0:T(8,128)(2,1)S(1)}, u32[]{:S(2)}, u32[]{:S(2)}) collective-permute-start(bf16[16,8192]{1,0:T(8,128)(2,1)S(1)} %get-tuple-element.56), channel_id=1, source_target_pairs={{0,4},{4,8},{8,12},{12,16},{16,20},{20,24},{24,28},{28,32},{32,36}... | collective-permute-start | bytes 786440 | tf_op jit(solution)/shard_map/ppermute | solution.py:15
  147.7 5.4 %collective-permute-start.5 = (bf16[16,8192]{1,0:T(8,128)(2,1)S(1)}, bf16[16,8192]{1,0:T(8,128)(2,1)S(1)}, u32[]{:S(2)}, u32[]{:S(2)}) collective-permute-start(bf16[16,8192]{1,0:T(8,128)(2,1)S(1)} %get-tuple-element.57), channel_id=1, source_target_pairs={{4,0},{8,4},{12,8},{16,12},{20,16},{24,20},{28,24},{32,28},{36,32}... | collective-permute-start | bytes 786440 | tf_op jit(solution)/shard_map/ppermute | solution.py:18
  159.3 3.0 copy-start.20
  162.3 2.0 copy-start.17
  164.3 2.0 copy-start.14
  182.2 13.9 %copy-start.18 = (s32[125,128]{0,1:T(8,128)S(1)}, s32[125,128]{0,1:T(8,128)}, u32[]{:S(2)}) copy-start(s32[125,128]{0,1:T(8,128)} %copy.68) | copy-start | bytes 192004
  196.1 12.7 %copy-start.12 = (f32[128,125,16]{1,2,0:T(8,128)S(1)}, f32[128,125,16]{1,2,0:T(8,128)}, u32[]{:S(2)}) copy-start(f32[128,125,16]{1,2,0:T(8,128)} %fusion.5) | copy-start | bytes 3072004
  208.7 2.6 copy-start.11
  213.9 5.7 %copy-start.15 = (s32[125,128]{0,1:T(8,128)S(1)}, s32[125,128]{0,1:T(8,128)}, u32[]{:S(2)}) copy-start(s32[125,128]{0,1:T(8,128)} %copy.73) | copy-start | bytes 192004
  232.7 11.2 %copy-start.6 = (f32[16,128,192]{2,0,1:T(8,128)S(1)}, f32[16,128,192]{2,0,1:T(8,128)}, u32[]{:S(2)}) copy-start(f32[16,128,192]{2,0,1:T(8,128)} %fusion.43) | copy-start | bytes 4718596
  232.7 11.2 %copy-start.7 = (f32[16,128,192]{2,0,1:T(8,128)S(1)}, f32[16,128,192]{2,0,1:T(8,128)}, u32[]{:S(2)}) copy-start(f32[16,128,192]{2,0,1:T(8,128)} %fusion.45) | copy-start | bytes 4718596
  254.7 10.9 %copy-start.3 = (bf16[16,32768]{1,0:T(8,128)(2,1)S(1)}, bf16[16,32768]{1,0:T(8,128)(2,1)}, u32[]{:S(2)}) copy-start(bf16[16,32768]{1,0:T(8,128)(2,1)} %param.12) | copy-start | bytes 3145732
  254.7 10.9 %copy-start.5 = (bf16[16,32768]{1,0:T(8,128)(2,1)S(1)}, bf16[16,32768]{1,0:T(8,128)(2,1)}, u32[]{:S(2)}) copy-start(bf16[16,32768]{1,0:T(8,128)(2,1)} %copy-done.4) | copy-start | bytes 3145732
  254.7 8.9 %collective-permute-start.6 = (bf16[16,8192]{1,0:T(8,128)(2,1)S(1)}, bf16[16,8192]{1,0:T(8,128)(2,1)S(1)}, u32[]{:S(2)}, u32[]{:S(2)}) collective-permute-start(bf16[16,8192]{1,0:T(8,128)(2,1)S(1)} %get-tuple-element.53), channel_id=1, source_target_pairs={{4,0},{8,4},{12,8},{16,12},{20,16},{24,20},{28,24},{32,28},{36,32}... | collective-permute-start | bytes 786440 | tf_op jit(solution)/shard_map/ppermute | solution.py:26
  256.3 8.4 %collective-permute-start.7 = (bf16[16,8192]{1,0:T(8,128)(2,1)S(1)}, bf16[16,8192]{1,0:T(8,128)(2,1)S(1)}, u32[]{:S(2)}, u32[]{:S(2)}) collective-permute-start(bf16[16,8192]{1,0:T(8,128)(2,1)S(1)} %get-tuple-element.52), channel_id=1, source_target_pairs={{0,4},{4,8},{8,12},{12,16},{16,20},{20,24},{24,28},{28,32},{32,36}... | collective-permute-start | bytes 786440 | tf_op jit(solution)/shard_map/ppermute | solution.py:26
  267.0 159.0 %all-gather.6.cloned.1.call-start = ((), (), s32[]{:S(2)}) async-start(), calls=%async_computation.1 | async-start | bytes 2129920 | tf_op jit(solution)/shard_map/all_gather | solution.py:106
Sparse Core Ops, SparseCore 0:
  267.1 75.0 all-gather.3
  347.7 78.2 all-gather.5
